TPU v7x, 32 devices: a whole 2x2x4 slice. The times are simulated.
32 devices in a mesh: table: 2 (over x), batch: 16 (over z, y, core).
Axes of the slice: x: 2, y: 2, z: 4, core: 2. Of those that a mesh axis runs over, the one named last changes fastest.
Arguments:
- x_first: bfloat16 [2048, 4096], P('batch', 'table'), may hold values from -6 to 6
- x_layer: bfloat16 [2048, 4096], P('batch', 'table'), may hold values from -6 to 6
- pre_act: bfloat16 [2048, 4096], P('batch', 'table'), may hold values from -8 to 8
- gamma: float32 [4096], P('table'), may hold values from 0.3 to 3
- weight: float32 [4096, 4096], P('table', 'batch'), may hold values from -0.09375 to 0.09375
- cotangent: bfloat16 [2048, 4096], P('batch', 'table'), may hold values from -12 to 12
Outputs:
- grad_first: bfloat16 [2048, 4096], P('batch', 'table')
- grad_layer: bfloat16 [2048, 4096], P('batch', 'table')
- grad_weight: float32 [4096, 4096], P('table', 'batch')
- grad_bias: float32 [4096], P('table')
- grad_gamma: float32 [4096], P('table')
All inputs are finite; a program needn't handle non-finite values.
Results may differ from a plain program's by a relative error of at most 0.005.
Values may be sent and summed in bfloat16 or wider, within the bound.
A program may use at most 128 MiB of HBM per device.

v0:
```python
import functools

import jax
import jax.numpy as jnp
from jax import lax
from jax.experimental import pallas as pl
from jax.experimental.pallas import tpu as pltpu
from jax.sharding import PartitionSpec as P

MESH = pl.DeviceIdType.MESH
F32 = jnp.float32
BF16 = jnp.bfloat16


def exchange(
    nb, parts,
    x_ref, act_ref, cot_ref, gamma_ref, cols_ref, weight_ref,
    first_ref, wsum_ref, ret_ref, total_ref,
    pre_ref, held, xall, mine, theirs, inbox, summed, layover, guest, small_ref, smalls, wfull, wbf,
    ring_send, ring_recv, sib_send, sib_recv, own_sem, x_send, x_on, x_recv, swap,
    pair_send, pair_recv, sum_send, lay_recv, lay_send, ret_recv, small_send, small_recv, w_sem,
):
    rows, outs = x_ref.shape
    per = nb // 2
    nc = nb // 2
    hops = nc // 2
    part = rows // parts
    t, b = lax.axis_index("table"), lax.axis_index("batch")
    q, c = b // 2, b % 2
    other = 1 - t

    def chip_at(p):
        p = (p + nc) % nc
        return jnp.where(p < hops, 2 * p, 2 * (nc - 1 - p) + 1)

    p = jnp.where(q % 2 == 0, q // 2, nc - 1 - q // 2)
    ahead = [2 * chip_at(p + 1) + c, 2 * chip_at(p - 1) + c]
    origin = lambda d, k: chip_at(p - k if d == 0 else p + k)
    count = lambda d, core: jnp.where(core == d, hops, hops - 1)
    home = b // per
    slot = b % per

    def piece(chip, core, h):
        return held.at[chip, pl.ds(pl.multiple_of(core * rows + h * part, part), part), :]

    def block(ref, bb):
        return ref.at[bb // 2, pl.ds(pl.multiple_of((bb % 2) * rows, rows), rows), :]

    def features(ref, j):
        cols = wfull.shape[1]
        return ref.at[j] if len(ref.shape) == 3 else ref.at[:, pl.ds(pl.multiple_of(j * cols, cols), cols)]

    def done(ref, sem):
        pltpu.make_async_copy(ref, ref, sem).wait()

    def send(src, dst, ssem, rsem, tt, bb):
        return pltpu.make_async_remote_copy(
            src_ref=src, dst_ref=dst, send_sem=ssem, recv_sem=rsem, device_id=(tt, bb), device_id_type=MESH
        ).start()

    def each(k, act):
        act(origin(0, k))

        @pl.when(jnp.logical_and(k > 0, k < hops))
        def _():
            act(origin(1, k))

    load_w = pltpu.make_async_copy(weight_ref, wfull, w_sem)
    load_w.start()
    barrier = pltpu.get_barrier_semaphore()

    def greet(i, carry):
        tt, bb = i // nb, i % nb

        @pl.when(jnp.logical_or(tt != t, bb != b))
        def _():
            pl.semaphore_signal(barrier, inc=1, device_id=(tt, bb), device_id_type=MESH)

        return carry

    lax.fori_loop(0, 2 * nb, greet, 0)
    small_ref[...] = jnp.zeros_like(small_ref)
    wide = 512 if outs % 512 == 0 else outs

    def gate(i, carry):
        at = pl.ds(pl.multiple_of(i * part, part), part)
        for lane in range(0, outs, wide):
            to = pl.ds(lane, wide)
            sharp = gamma_ref[:, to]
            act = act_ref[at, to].astype(F32)
            cot = cot_ref[at, to].astype(F32)
            tanh = jnp.tanh(sharp * act)
            hidden = cot * x_ref[at, to].astype(F32)
            slope = 1.0 - tanh * tanh
            first_ref[at, to] = (cot * (act * tanh)).astype(BF16)
            pre = (hidden * (tanh + sharp * act * slope)).astype(BF16)
            pre_ref[at, to] = pre
            small_ref[0:1, to] += jnp.sum(pre.astype(F32), axis=0, keepdims=True)
            small_ref[1:2, to] += jnp.sum(hidden * act * act * slope, axis=0, keepdims=True)
        return carry

    lax.fori_loop(0, parts, gate, 0)
    pl.semaphore_wait(barrier, 2 * nb - 1)

    for h in range(parts):
        start = pre_ref.at[pl.ds(h * part, part), :]
        for d in range(2):
            @pl.when(count(d, c) > 0)
            def _():
                send(start, piece(q, c, h), ring_send.at[d, 0, h], ring_recv.at[d, 0, h], t, ahead[d])
    send(pre_ref, block(held, b), own_sem.at[0], own_sem.at[1], t, 2 * q + 1 - c)
    own_copy = pltpu.make_async_copy(pre_ref, block(held, b), own_sem.at[2])
    own_copy.start()

    odd = b % 2 == 1
    side = jnp.where(odd, other, t)

    def give_columns(source):
        def give(j, carry):
            at = (j + slot) % per
            bb = side * per + at

            @pl.when(bb == b)
            def _():
                pltpu.make_async_copy(features(source, at), block(xall, b), x_recv.at[b]).start()

            @pl.when(bb != b)
            def _():
                send(features(source, at), block(xall, b), x_send.at[at], x_recv.at[b], t, bb)

            return carry

        lax.fori_loop(0, per, give, 0)

    @pl.when(odd)
    def _():
        send(cols_ref, guest, swap.at[0], swap.at[1], other, b)

    @pl.when(jnp.logical_not(odd))
    def _():
        give_columns(cols_ref)

    def give_small(bb, carry):
        @pl.when(bb != b)
        def _():
            send(small_ref, smalls.at[b], small_send.at[bb], small_recv.at[b], t, bb)

        return carry

    lax.fori_loop(0, nb, give_small, 0)
    load_w.wait()
    wbf[...] = wfull[...].astype(BF16)
    wsum_ref[...] = jnp.zeros_like(wsum_ref)

    def lands_here(bb):
        return (home + bb) % 2 == t

    def pass_columns(chip):
        for core in range(2):
            bb = 2 * chip + core

            @pl.when(lands_here(bb))
            def _():
                done(block(xall, bb), x_recv.at[bb])
                send(block(xall, bb), block(xall, bb), x_on.at[bb], x_recv.at[bb], other, b)

    def half(chip, which):
        at = pl.ds(pl.multiple_of(which * rows, rows), rows)
        return jnp.dot(held[chip, at, :], wbf[...], preferred_element_type=F32)

    def multiply(chip):
        theirs[chip] = half(chip, other).astype(BF16)
        send(theirs.at[chip], inbox.at[chip], pair_send.at[chip], pair_recv.at[chip], other, b)
        mine[chip] = half(chip, t)

    def give_sum(chip):
        done(inbox.at[chip], pair_recv.at[chip])
        summed[chip] = (mine[chip] + inbox[chip].astype(F32)).astype(BF16)
        bb = 2 * chip + t
        for stays, dst, rsem in ((True, ret_ref, ret_recv), (False, layover, lay_recv)):
            right = (home == t) if stays else (home != t)

            @pl.when(jnp.logical_and(right, bb == b))
            def _():
                pltpu.make_async_copy(summed.at[chip], features(dst, slot), rsem.at[slot]).start()

            @pl.when(jnp.logical_and(right, bb != b))
            def _():
                send(summed.at[chip], features(dst, slot), sum_send.at[chip], rsem.at[slot], t, bb)

    def pass_sum(chip):
        for core in range(2):
            bb = 2 * chip + core
            j = bb % per

            @pl.when(jnp.logical_and(c == t, bb // per != t))
            def _():
                done(layover.at[j], lay_recv.at[j])
                send(layover.at[j], features(ret_ref, j), lay_send.at[j], ret_recv.at[j], other, b)

    def add_weight(chip):
        for core in range(2):
            bb = 2 * chip + core

            @pl.when(jnp.logical_not(lands_here(bb)))
            def _():
                done(block(xall, bb), x_recv.at[bb])

        def step(i, carry):
            at = pl.ds(pl.multiple_of(i * wide, wide), wide)
            wsum_ref[at, :] += lax.dot_general(
                held[chip, :, at], xall[chip], (((0,), (0,)), ((), ())), preferred_element_type=F32
            )
            return carry

        lax.fori_loop(0, outs // wide, step, 0)

    own_copy.wait()
    done(block(held, b), own_sem.at[1])
    multiply(q)

    @pl.when(odd)
    def _():
        done(guest, swap.at[1])
        give_columns(guest)

    pass_columns(q)

    def hop(k, carry):
        for h in range(parts):
            for d in range(2):
                here = piece(origin(d, k + 1), c, h)

                @pl.when(k < count(d, c))
                def _():
                    done(here, ring_recv.at[d, k, h])

                    @pl.when(k + 1 < count(d, c))
                    def _():
                        send(here, here, ring_send.at[d, k + 1, h], ring_recv.at[d, k + 1, h], t, ahead[d])

                    send(here, here, sib_send.at[d, k, h], sib_recv.at[d, k, h], t, 2 * q + 1 - c)
        each(k, give_sum)
        each(k + 1, pass_columns)
        for d in range(2):
            @pl.when(k < count(d, 1 - c))
            def _():
                for h in range(parts):
                    done(piece(origin(d, k + 1), 1 - c, h), sib_recv.at[d, k, h])
        each(k + 1, multiply)

        @pl.when(k > 0)
        def _():
            each(k - 1, pass_sum)

        each(k, add_weight)
        return carry

    lax.fori_loop(0, hops, hop, 0)
    each(hops, give_sum)
    each(hops - 1, pass_sum)
    each(hops, add_weight)
    each(hops, pass_sum)

    smalls[b] = small_ref[...]

    def take_small(bb, carry):
        @pl.when(bb != b)
        def _():
            done(smalls.at[bb], small_recv.at[bb])
            done(small_ref, small_send.at[bb])

        return carry

    lax.fori_loop(0, nb, take_small, 0)
    total_ref[...] = jnp.sum(smalls[...], axis=0)

    @pl.when(odd)
    def _():
        done(cols_ref, swap.at[0])

    def sent_columns(j, carry):
        @pl.when(side * per + j != b)
        def _():
            done(features(cols_ref, j), x_send.at[j])

        return carry

    lax.fori_loop(0, per, sent_columns, 0)

    def sent_on(bb, carry):
        @pl.when(lands_here(bb))
        def _():
            done(block(xall, bb), x_on.at[bb])

        return carry

    lax.fori_loop(0, nb, sent_on, 0)

    def sent_sums(chip, carry):
        done(theirs.at[chip], pair_send.at[chip])

        @pl.when(2 * chip + t != b)
        def _():
            done(summed.at[chip], sum_send.at[chip])

        return carry

    lax.fori_loop(0, nc, sent_sums, 0)

    def came(j, carry):
        done(features(ret_ref, j), ret_recv.at[j])

        @pl.when(c == t)
        def _():
            done(layover.at[j], lay_send.at[j])

        return carry

    lax.fori_loop(0, per, came, 0)
    done(pre_ref, own_sem.at[0])

    def sent_pieces(k, carry):
        for h in range(parts):
            for d in range(2):
                @pl.when(k < count(d, c))
                def _():
                    done(piece(origin(d, k), c, h), ring_send.at[d, k, h])
                    done(piece(origin(d, k + 1), c, h), sib_send.at[d, k, h])

        return carry

    lax.fori_loop(0, hops, sent_pieces, 0)


def run_exchange(nb, x_first, pre_act, cotangent, gamma, columns, weight):
    rows, outs = x_first.shape
    cols = weight.shape[1]
    nc, per, hops = nb // 2, nb // 2, nb // 4
    parts = 8 if rows % 128 == 0 else 4 if rows % 64 == 0 else 1
    dma = pltpu.SemaphoreType.DMA
    vmem = pl.BlockSpec(memory_space=pltpu.VMEM)
    return pl.pallas_call(
        functools.partial(exchange, nb, parts),
        out_shape=(
            jax.ShapeDtypeStruct((rows, outs), BF16),
            jax.ShapeDtypeStruct((outs, cols), F32),
            jax.ShapeDtypeStruct(columns.shape, BF16),
            jax.ShapeDtypeStruct((2, outs), F32),
        ),
        in_specs=[vmem] * 5 + [pl.BlockSpec(memory_space=pl.ANY)],
        out_specs=(vmem,) * 4,
        scratch_shapes=[
            pltpu.VMEM((rows, outs), BF16),
            pltpu.VMEM((nc, 2 * rows, outs), BF16),
            pltpu.VMEM((nc, 2 * rows, cols), BF16),
            pltpu.VMEM((nc, rows, cols), F32),
            pltpu.VMEM((nc, rows, cols), BF16),
            pltpu.VMEM((nc, rows, cols), BF16),
            pltpu.VMEM((nc, rows, cols), BF16),
            pltpu.VMEM((per, rows, cols), BF16),
            pltpu.VMEM(columns.shape, BF16),
            pltpu.VMEM((2, outs), F32),
            pltpu.VMEM((nb, 2, outs), F32),
            pltpu.VMEM((outs, cols), F32),
            pltpu.VMEM((outs, cols), BF16),
            dma((2, hops, parts)),
            dma((2, hops, parts)),
            dma((2, hops, parts)),
            dma((2, hops, parts)),
            dma((3,)),
            dma((per,)),
            dma((nb,)),
            dma((nb,)),
            dma((2,)),
            dma((nc,)),
            dma((nc,)),
            dma((nc,)),
            dma((per,)),
            dma((per,)),
            dma((per,)),
            dma((nb,)),
            dma((nb,)),
            dma,
        ],
        compiler_params=pltpu.CompilerParams(
            collective_id=0, has_side_effects=True, vmem_limit_bytes=60 * 1024 * 1024
        ),
    )(x_first, pre_act, cotangent, gamma, columns, weight)


def shards(nb, x_first, x_layer, pre_act, gamma, weight, cotangent):
    rows = x_layer.shape[0]
    per, cols = nb // 2, weight.shape[1]
    aligned = cols % 128 == 0
    columns = x_layer if aligned else x_layer.reshape(rows, per, cols).transpose(1, 0, 2)
    grad_first, grad_weight, share, total = run_exchange(
        nb, x_first, pre_act, cotangent, gamma[None], columns, weight
    )
    if not aligned:
        share = share.transpose(1, 0, 2).reshape(rows, per * cols)
    grad_layer = (cotangent.astype(F32) + share.astype(F32)).astype(BF16)
    return (grad_first, grad_layer, grad_weight, total[0], total[1])


def solution(mesh):
    assert mesh.shape["table"] == 2 and mesh.shape["batch"] % 4 == 0
    placed = (
        P("batch", "table"),
        P("batch", "table"),
        P("batch", "table"),
        P("table"),
        P("table", "batch"),
        P("batch", "table"),
    )
    return jax.shard_map(
        functools.partial(shards, mesh.shape["batch"]),
        mesh=mesh,
        in_specs=placed,
        out_specs=(
            P("batch", "table"),
            P("batch", "table"),
            P("table", "batch"),
            P("table"),
            P("table"),
        ),
        check_vma=False,
    )
```

profile of v0, /device:TPU:14, one launch (start us, length us, event | category | flops | bytes accessed | tf_op | source)
XLA Modules:
  0.0 96.3 jit_solution(15157914418520278301)
XLA Ops:
  0.6 0.0 copy-start.1
  0.6 88.9 %shard_map.101 = (bf16[128,2048]{1,0:T(8,128)(2,1)}, f32[2048,256]{1,0:T(8,128)}, bf16[128,2048]{1,0:T(8,128)(2,1)}, f32[2,2048]{1,0:T(2,128)}) custom-call(bf16[128,2048]{1,0:T(8,128)(2,1)} %x_ref.1, bf16[128,2048]{1,0:T(8,128)(2,1)} %act_ref.1, bf16[128,2048]{1,0:T(8,128)(2,1)} %cot_ref.1, f32[1,2048]{1,0:T(1,128)} %bitcast.3, bf16[128,2048]{1,0:T(8,128)(2,1)} %cols_ref.1, ...), custom_call_target="tpu_custom_call" | custom-call | tf_op jit(solution)/shard_map/pallas_call | solution.py:343
  89.6 0.0 copy-start
  89.6 1.5 %fusion = (f32[1,2048]{1,0:T(1,128)}, f32[1,2048]{1,0:T(1,128)}) fusion(f32[2,2048]{1,0:T(2,128)} %get-tuple-element.12), kind=kLoop, calls=%fused_computation.1 | loop fusion | bytes 32768 | tf_op jit(solution)/shard_map/slice | solution.py:403
  91.1 0.0 copy-done.1
  91.1 2.0 %add_convert_fusion = bf16[128,2048]{1,0:T(8,128)(2,1)} fusion(bf16[128,2048]{1,0:T(8,128)(2,1)} %get-tuple-element.10, bf16[128,2048]{1,0:T(8,128)(2,1)S(1)} %copy-done.1), kind=kLoop, calls=%fused_computation | loop fusion | flops 1048576 | bytes 1572864 | tf_op jit(solution)/shard_map/convert_element_type | solution.py:402
  93.1 1.9 %copy.13 = bf16[128,2048]{1,0:T(8,128)(2,1)} copy(bf16[128,2048]{1,0:T(8,128)(2,1)} %get-tuple-element.20) | data formatting | bytes 1048576
  94.9 0.0 copy-done
  94.9 1.3 %copy.14 = f32[2048,256]{1,0:T(8,128)} copy(f32[2048,256]{1,0:T(8,128)S(1)} %copy-done) | data formatting | bytes 4194304
Async XLA Ops:
  0.6 90.5 %copy-start.1 = (bf16[128,2048]{1,0:T(8,128)(2,1)S(1)}, bf16[128,2048]{1,0:T(8,128)(2,1)}, u32[]{:S(2)}) copy-start(bf16[128,2048]{1,0:T(8,128)(2,1)} %cot_ref.1) | copy-start | bytes 1572868
  89.6 5.4 %copy-start = (f32[2048,256]{1,0:T(8,128)S(1)}, f32[2048,256]{1,0:T(8,128)}, u32[]{:S(2)}) copy-start(f32[2048,256]{1,0:T(8,128)} %get-tuple-element.22) | copy-start | bytes 6291460
where the time goes:
time: 96.5 us; the launch traced here: 96.3 us
  Pallas kernels  88.9 us (92%)
  local copies, waits for them, and re-layouts  4.7 us (5%)
  other arithmetic  1.96 us (2%)
    pallas_call x1, Pallas kernels, run_exchange(): pl.pallas_call(functools.partial(exchange, nb, parts), out_shape=(jax.Sha...  88.9 us
    unnamed x6, local copies, waits for them, and re-layouts  3.21 us
    convert_element_type x1, other arithmetic, shards(): grad_layer = (cotangent.astype(F32) + share.astype(F32)).astype(BF16)  1.96 us

commit v1 on v0

v1 whole, which is shorter than its diff:
```python
import functools

import jax
import jax.numpy as jnp
from jax import lax
from jax.experimental import pallas as pl
from jax.experimental.pallas import tpu as pltpu
from jax.sharding import PartitionSpec as P

MESH = pl.DeviceIdType.MESH
F32 = jnp.float32
BF16 = jnp.bfloat16


def exchange(
    nb, phases, parts,
    x_ref, act_ref, cot_ref, gamma_ref, cols_ref, weight_ref,
    wsum_ref, ret_ref, total_ref,
    held, xall, mine, theirs, inbox, summed, layover, guest, small_ref, smalls, half_ref, away_ref,
    wfull, wbf, wsend, winbox,
    line_send, line_recv, sib_send, sib_recv, own_sem, w_sem, x_send, x_on, x_recv, swap,
    pair_send, pair_recv, sum_send, lay_recv, lay_send, ret_recv, small_send, small_recv, away_sem,
    share_send, share_recv, load_sem,
):
    rows, outs = x_ref.shape
    cols = wfull.shape[1]
    nz, per = nb // 4, nb // 2
    hz, last = nz // 2, nz - 1
    chunks = phases * parts
    wide = outs // chunks
    t, b = lax.axis_index("table"), lax.axis_index("batch")
    z, y, c = b // 4, (b // 2) % 2, b % 2
    other = 1 - t
    home = z // hz

    def device(zz, yy, cc):
        return (zz * 2 + yy) * 2 + cc

    def column(zz, yy, cc):
        return ((zz % hz) * 2 + yy) * 2 + cc

    sibling, across = device(z, y, 1 - c), device(z, 1 - y, c)
    came = (z, last - z)
    goes = (z < last, z > 0)
    ahead = (b + 4, b - 4)

    def origin(d, k):
        return z - 1 - k if d == 0 else z + 1 + k

    def core_rows(core):
        return pl.ds(pl.multiple_of(core * rows, rows), rows)

    def piece(zz, core, chunk):
        return held.at[zz, core_rows(core), pl.ds(chunk * wide, wide)]

    def xblock(yy, zz, core):
        return xall.at[yy, zz, core_rows(core), :]

    def features(ref, j):
        return ref.at[j] if len(ref.shape) == 3 else ref.at[:, pl.ds(pl.multiple_of(j * cols, cols), cols)]

    def done(ref, sem):
        pltpu.make_async_copy(ref, ref, sem).wait()

    def send(src, dst, ssem, rsem, tt, bb):
        return pltpu.make_async_remote_copy(
            src_ref=src, dst_ref=dst, send_sem=ssem, recv_sem=rsem, device_id=(tt, bb), device_id_type=MESH
        ).start()

    def each(k, act):
        for d in range(2):
            @pl.when(k < came[d])
            def _():
                act(origin(d, k))

    load_w = pltpu.make_async_copy(weight_ref, wfull, load_sem)
    load_w.start()
    barrier = pltpu.get_barrier_semaphore()

    def greet(tt, bb):
        pl.semaphore_signal(barrier, inc=1, device_id=(tt, bb), device_id_type=MESH)

    greet(other, b)
    greet(t, across)

    def along(act):
        def step(i, carry):
            bb = device(i // 2, y, i % 2)

            @pl.when(bb != b)
            def _():
                act(i, bb)

            return carry

        lax.fori_loop(0, 2 * nz, step, 0)

    along(lambda i, bb: greet(t, bb))
    small_ref[...] = jnp.zeros_like(small_ref)
    tall = 16 if rows % 16 == 0 else rows
    lanes = 512 if outs % 512 == 0 else outs

    def gate(i, carry):
        at = pl.ds(pl.multiple_of(i * tall, tall), tall)
        put = pl.ds(pl.multiple_of(c * rows + i * tall, tall), tall)
        for lane in range(0, outs, lanes):
            to = pl.ds(lane, lanes)
            sharp = gamma_ref[:, to]
            act = act_ref[at, to].astype(F32)
            tanh = jnp.tanh(sharp * act)
            hidden = cot_ref[at, to].astype(F32) * x_ref[at, to].astype(F32)
            slope = 1.0 - tanh * tanh
            pre = (hidden * (tanh + sharp * act * slope)).astype(BF16)
            held[z, put, to] = pre
            small_ref[0:1, to] += jnp.sum(pre.astype(F32), axis=0, keepdims=True)
            small_ref[1:2, to] += jnp.sum(hidden * act * act * slope, axis=0, keepdims=True)
        return carry

    lax.fori_loop(0, rows // tall, gate, 0)
    load_w.wait()
    wbf[y] = wfull[...].astype(BF16)
    pl.semaphore_wait(barrier, 2 * nz + 1)

    def give_own(d, phase):
        @pl.when(goes[d])
        def _():
            for chunk in range(phase * parts, phase * parts + parts):
                here = piece(z, c, chunk)
                send(here, here, line_send.at[d, 0, chunk], line_recv.at[d, 0, chunk], t, ahead[d])

    give_own(0, 0)
    give_own(1, 0)
    own_rows = held.at[z, core_rows(c), :]
    send(own_rows, own_rows, own_sem.at[0], own_sem.at[1], t, sibling)
    send(wbf.at[y], wbf.at[y], w_sem.at[0], w_sem.at[1], t, across)

    odd = c == 1
    side = jnp.where(odd, other, t)

    def target(j):
        return device(side * hz + j // 4, y, j % 2)

    def give_columns(source):
        def give(i, carry):
            j = (i + column(z, 0, c)) % per
            bb = target(j)
            there = xblock((j // 2) % 2, z, c)
            rsem = x_recv.at[(j // 2) % 2, z, c]

            @pl.when(bb == b)
            def _():
                pltpu.make_async_copy(features(source, j), there, rsem).start()

            @pl.when(bb != b)
            def _():
                send(features(source, j), there, x_send.at[j], rsem, t, bb)

            return carry

        lax.fori_loop(0, per, give, 0)

    @pl.when(odd)
    def _():
        send(cols_ref, guest, swap.at[0], swap.at[1], other, b)

    @pl.when(jnp.logical_not(odd))
    def _():
        give_columns(cols_ref)

    along(lambda i, bb: send(small_ref, smalls.at[2 * z + c], small_send.at[i], small_recv.at[2 * z + c], t, bb))
    smalls[2 * z + c] = small_ref[...]
    lands = (home + t) % 2

    def pass_columns(zz):
        for yy in range(2):
            ref = xblock(yy, zz, lands)
            done(ref, x_recv.at[yy, zz, lands])
            send(ref, ref, x_on.at[yy, zz], x_recv.at[yy, zz, lands], other, b)

    def take_columns():
        def step(zz, carry):
            for yy in range(2):
                done(xblock(yy, zz, 1 - lands), x_recv.at[yy, zz, 1 - lands])
            return carry

        lax.fori_loop(0, nz, step, 0)

    def half(zz, which, yy):
        return jnp.dot(held[zz, core_rows(which), :], wbf[yy], preferred_element_type=F32)

    def multiply(zz):
        for yy in range(2):
            theirs[zz, yy] = half(zz, other, yy).astype(BF16)
        send(theirs.at[zz], inbox.at[zz], pair_send.at[zz], pair_recv.at[zz], other, b)
        for yy in range(2):
            mine[zz, yy] = half(zz, t, yy)

    def give_sum(zz):
        done(inbox.at[zz], pair_recv.at[zz])
        summed[zz] = (mine[zz] + inbox[zz].astype(F32)).astype(BF16)
        bb = device(zz, y, t)
        for yy in range(2):
            slot = column(z, yy, c)
            for stays, dst, rsem in ((True, ret_ref, ret_recv), (False, layover, lay_recv)):
                right = (home == t) if stays else (home != t)

                @pl.when(jnp.logical_and(right, bb == b))
                def _():
                    pltpu.make_async_copy(summed.at[zz, yy], features(dst, slot), rsem.at[slot]).start()

                @pl.when(jnp.logical_and(right, bb != b))
                def _():
                    send(summed.at[zz, yy], features(dst, slot), sum_send.at[zz, yy], rsem.at[slot], t, bb)

    def pass_sum(zz):
        @pl.when(jnp.logical_and(c == t, zz // hz != t))
        def _():
            for yy in range(2):
                for cc in range(2):
                    j = column(zz, yy, cc)
                    done(layover.at[j], lay_recv.at[j])
                    send(layover.at[j], features(ret_ref, j), lay_send.at[j], ret_recv.at[j], other, b)

    group = 4 if nz % 4 == 0 else nz

    def product(chunk, yy):
        to = pl.ds(chunk * wide, wide)
        total = None
        for g in range(0, nz, group):
            zs = pl.ds(g, group)
            term = lax.dot_general(
                held[zs, :, to].reshape(group * 2 * rows, wide),
                xall[yy, zs].reshape(group * 2 * rows, cols),
                (((0,), (0,)), ((), ())),
                preferred_element_type=F32,
            )
            total = term if total is None else total + term
        return total

    def give_share(chunk):
        wsend[chunk] = product(chunk, 1 - y).astype(BF16)
        send(wsend.at[chunk], winbox.at[chunk], share_send.at[chunk], share_recv.at[chunk], t, across)

    def keep_share(chunk):
        wsum_ref[pl.ds(chunk * wide, wide), :] = product(chunk, y)

    def hop(phase, k):
        for chunk in range(phase * parts, phase * parts + parts):
            for d in range(2):
                @pl.when(k < came[d])
                def _():
                    here = piece(origin(d, k), c, chunk)
                    done(here, line_recv.at[d, k, chunk])

                    @pl.when(goes[d])
                    def _():
                        send(here, here, line_send.at[d, k + 1, chunk], line_recv.at[d, k + 1, chunk], t, ahead[d])

                    send(here, here, sib_send.at[d, k, chunk], sib_recv.at[d, k, chunk], t, sibling)

        if phase + 1 < phases:
            for d in range(2):
                @pl.when(k == came[d])
                def _():
                    give_own(d, phase + 1)

    def meet(phase, k):
        for d in range(2):
            @pl.when(k < came[d])
            def _():
                for chunk in range(phase * parts, phase * parts + parts):
                    done(piece(origin(d, k), 1 - c, chunk), sib_recv.at[d, k, chunk])

    for phase in range(phases - 1):
        def gather(k, carry):
            hop(phase, k)
            if phase == 0:
                @pl.when(k == 0)
                def _():
                    @pl.when(odd)
                    def _():
                        done(guest, swap.at[1])
                        give_columns(guest)

                    pass_columns(z)

                each(k, pass_columns)
            meet(phase, k)
            return carry

        lax.fori_loop(0, last, gather, 0)
    along(lambda i, bb: done(smalls.at[i], small_recv.at[i]))
    half_ref[...] = jnp.sum(smalls[...], axis=0)
    send(half_ref, away_ref, away_sem.at[0], away_sem.at[1], t, across)
    theirs_rows = held.at[z, core_rows(1 - c), :]
    done(theirs_rows, own_sem.at[1])
    done(wbf.at[1 - y], w_sem.at[1])
    multiply(z)

    early = chunks - parts

    def finish(k, carry):
        hop(phases - 1, k)
        meet(phases - 1, k)
        each(k, multiply)

        @pl.when(k == 0)
        def _():
            give_sum(z)
            take_columns()

        @pl.when(k > 0)
        def _():
            each(k - 1, give_sum)

        @pl.when(k == 1)
        def _():
            pass_sum(z)

        @pl.when(k > 1)
        def _():
            each(k - 2, pass_sum)

        for chunk in range(early):
            @pl.when(k == min(chunk, last - 1))
            def _():
                give_share(chunk)
                keep_share(chunk)

        return carry

    lax.fori_loop(0, last, finish, 0)
    for chunk in range(early, chunks):
        give_share(chunk)
    each(last - 1, give_sum)
    if last == 1:
        pass_sum(z)
    else:
        each(last - 2, pass_sum)
    for chunk in range(early, chunks):
        keep_share(chunk)
    each(last - 1, pass_sum)
    for chunk in range(chunks):
        done(winbox.at[chunk], share_recv.at[chunk])
        wsum_ref[pl.ds(chunk * wide, wide), :] += winbox[chunk].astype(F32)
    done(away_ref, away_sem.at[1])
    total_ref[...] = half_ref[...] + away_ref[...]

    along(lambda i, bb: done(small_ref, small_send.at[i]))
    done(half_ref, away_sem.at[0])
    done(own_rows, own_sem.at[0])
    done(wbf.at[y], w_sem.at[0])
    for chunk in range(chunks):
        done(wsend.at[chunk], share_send.at[chunk])

    @pl.when(odd)
    def _():
        done(cols_ref, swap.at[0])

    def sent_columns(j, carry):
        @pl.when(target(j) != b)
        def _():
            done(features(cols_ref, j), x_send.at[j])

        return carry

    lax.fori_loop(0, per, sent_columns, 0)

    def sent_line(zz, carry):
        for yy in range(2):
            done(xblock(yy, zz, lands), x_on.at[yy, zz])

            @pl.when(device(zz, y, t) != b)
            def _():
                done(summed.at[zz, yy], sum_send.at[zz, yy])

        done(theirs.at[zz], pair_send.at[zz])
        return carry

    lax.fori_loop(0, nz, sent_line, 0)

    def back(j, carry):
        done(features(ret_ref, j), ret_recv.at[j])

        @pl.when(c == t)
        def _():
            done(layover.at[j], lay_send.at[j])

        return carry

    lax.fori_loop(0, per, back, 0)

    def sent_pieces(k, carry):
        for chunk in range(chunks):
            for d in range(2):
                @pl.when(jnp.logical_and(goes[d], k <= came[d]))
                def _():
                    done(piece(z, c, chunk), line_send.at[d, k, chunk])

                @pl.when(k < came[d])
                def _():
                    done(piece(z, c, chunk), sib_send.at[d, k, chunk])

        return carry

    lax.fori_loop(0, last, sent_pieces, 0)


def run_exchange(nb, x_first, pre_act, cotangent, gamma, columns, weight):
    rows, outs = x_first.shape
    cols = weight.shape[1]
    nz, per = nb // 4, nb // 2
    last = nz - 1
    phases, parts = 2, 2
    chunks = phases * parts
    wide = outs // chunks
    dma = pltpu.SemaphoreType.DMA
    vmem = pl.BlockSpec(memory_space=pltpu.VMEM)
    return pl.pallas_call(
        functools.partial(exchange, nb, phases, parts),
        out_shape=(
            jax.ShapeDtypeStruct((outs, cols), F32),
            jax.ShapeDtypeStruct(columns.shape, BF16),
            jax.ShapeDtypeStruct((2, outs), F32),
        ),
        in_specs=[vmem] * 5 + [pl.BlockSpec(memory_space=pl.ANY)],
        out_specs=(vmem,) * 3,
        scratch_shapes=[
            pltpu.VMEM((nz, 2 * rows, outs), BF16),
            pltpu.VMEM((2, nz, 2 * rows, cols), BF16),
            pltpu.VMEM((nz, 2, rows, cols), F32),
            pltpu.VMEM((nz, 2, rows, cols), BF16),
            pltpu.VMEM((nz, 2, rows, cols), BF16),
            pltpu.VMEM((nz, 2, rows, cols), BF16),
            pltpu.VMEM((per, rows, cols), BF16),
            pltpu.VMEM(columns.shape, BF16),
            pltpu.VMEM((2, outs), F32),
            pltpu.VMEM((2 * nz, 2, outs), F32),
            pltpu.VMEM((2, outs), F32),
            pltpu.VMEM((2, outs), F32),
            pltpu.VMEM((outs, cols), F32),
            pltpu.VMEM((2, outs, cols), BF16),
            pltpu.VMEM((chunks, wide, cols), BF16),
            pltpu.VMEM((chunks, wide, cols), BF16),
            dma((2, last, chunks)),
            dma((2, last, chunks)),
            dma((2, last, chunks)),
            dma((2, last, chunks)),
            dma((2,)),
            dma((2,)),
            dma((per,)),
            dma((2, nz)),
            dma((2, nz, 2)),
            dma((2,)),
            dma((nz,)),
            dma((nz,)),
            dma((nz, 2)),
            dma((per,)),
            dma((per,)),
            dma((per,)),
            dma((2 * nz,)),
            dma((2 * nz,)),
            dma((2,)),
            dma((chunks,)),
            dma((chunks,)),
            dma,
        ],
        compiler_params=pltpu.CompilerParams(
            collective_id=0, has_side_effects=True, vmem_limit_bytes=60 * 1024 * 1024
        ),
    )(x_first, pre_act, cotangent, gamma, columns, weight)


def results(act_ref, cot_ref, gamma_ref, share_ref, wsum_ref, total_ref, first_ref, layer_ref, weight_ref, bias_ref, sharp_ref):
    act = act_ref[...].astype(F32)
    cot = cot_ref[...].astype(F32)
    first_ref[...] = (cot * (act * jnp.tanh(gamma_ref[...] * act))).astype(BF16)
    layer_ref[...] = (cot + share_ref[...].astype(F32)).astype(BF16)
    weight_ref[...] = wsum_ref[...]
    bias_ref[...] = total_ref[0:1, :]
    sharp_ref[...] = total_ref[1:2, :]


def write_results(pre_act, cotangent, gamma, share, wsum, total):
    rows, outs = pre_act.shape
    cols = wsum.shape[1]
    steps = 4 if rows % 64 == 0 and outs % 32 == 0 else 1
    some = pl.BlockSpec((rows // steps, outs), lambda i: (i, 0))
    tile = pl.BlockSpec((outs // steps, cols), lambda i: (i, 0))
    whole = lambda n: pl.BlockSpec((n, outs), lambda i: (0, 0))
    wide = jax.ShapeDtypeStruct((rows, outs), BF16)
    flat = jax.ShapeDtypeStruct((1, outs), F32)
    return pl.pallas_call(
        results,
        grid=(steps,),
        out_shape=(wide, wide, jax.ShapeDtypeStruct((outs, cols), F32), flat, flat),
        in_specs=[some, some, whole(1), some, tile, whole(2)],
        out_specs=(some, some, tile, whole(1), whole(1)),
    )(pre_act, cotangent, gamma, share, wsum, total)


def shards(nb, x_first, x_layer, pre_act, gamma, weight, cotangent):
    rows = x_layer.shape[0]
    per, cols = nb // 2, weight.shape[1]
    aligned = cols % 128 == 0
    columns = x_layer if aligned else x_layer.reshape(rows, per, cols).transpose(1, 0, 2)
    wsum, share, total = run_exchange(nb, x_first, pre_act, cotangent, gamma[None], columns, weight)
    if not aligned:
        share = share.transpose(1, 0, 2).reshape(rows, per * cols)
    first, layer, grad_weight, bias, sharp = write_results(pre_act, cotangent, gamma[None], share, wsum, total)
    return (first, layer, grad_weight, bias[0], sharp[0])


def solution(mesh):
    assert mesh.shape["table"] == 2 and mesh.shape["batch"] % 8 == 0
    placed = (
        P("batch", "table"),
        P("batch", "table"),
        P("batch", "table"),
        P("table"),
        P("table", "batch"),
        P("batch", "table"),
    )
    return jax.shard_map(
        functools.partial(shards, mesh.shape["batch"]),
        mesh=mesh,
        in_specs=placed,
        out_specs=(
            P("batch", "table"),
            P("batch", "table"),
            P("table", "batch"),
            P("table"),
            P("table"),
        ),
        check_vma=False,
    )
```

time: 96.5 us -> 84 us (0.87)
  the two profiles are of different devices: /device:TPU:14 before, /device:TPU:3 now
where the time goes in v1:
time: 84 us; the launch traced here: 83.8 us
  Pallas kernels  83.1 us (99%)
    pallas_call x1, Pallas kernels, run_exchange(): pl.pallas_call(functools.partial(exchange, nb, phases, parts), out_shape=...  78.8 us
    pallas_call x1, Pallas kernels, write_results(): pl.pallas_call(results, grid=(steps,), out_shape=(wide, wide, jax.ShapeDt...  4.37 us

profile of v1, /device:TPU:3, one launch (start us, length us, event | category | flops | bytes accessed | tf_op | source)
XLA Modules:
  0.0 83.8 jit_solution(9755853537588579863)
XLA Ops:
  0.6 78.8 %shard_map.101 = (f32[2048,256]{1,0:T(8,128)}, bf16[128,2048]{1,0:T(8,128)(2,1)}, f32[2,2048]{1,0:T(2,128)}) custom-call(bf16[128,2048]{1,0:T(8,128)(2,1)} %x_ref.1, bf16[128,2048]{1,0:T(8,128)(2,1)} %act_ref.3, bf16[128,2048]{1,0:T(8,128)(2,1)} %cot_ref.3, f32[1,2048]{1,0:T(1,128)} %bitcast.3, bf16[128,2048]{1,0:T(8,128)(2,1)} %cols_ref.1, ...), custom_call_target="tpu_custom_call" | custom-call | tf_op jit(solution)/shard_map/pallas_call | solution.py:419
  79.4 4.4 %shard_map.102 = (bf16[128,2048]{1,0:T(8,128)(2,1)}, bf16[128,2048]{1,0:T(8,128)(2,1)}, f32[2048,256]{1,0:T(8,128)}, f32[1,2048]{1,0:T(1,128)}, f32[1,2048]{1,0:T(1,128)}) custom-call(bf16[128,2048]{1,0:T(8,128)(2,1)} %act_ref.3, bf16[128,2048]{1,0:T(8,128)(2,1)} %cot_ref.3, f32[1,2048]{1,0:T(1,128)} %bitcast.4, ...), custom_call_target="tpu_custom_call" | custom-call | tf_op jit(solution)/shard_map/pallas_call | solution.py:493

commit v2 on v1

--- a/solution.py
+++ b/solution.py
@@ -13,21 +13,22 @@
 
 
 def exchange(
-    nb, phases, parts,
-    x_ref, act_ref, cot_ref, gamma_ref, cols_ref, weight_ref,
-    wsum_ref, ret_ref, total_ref,
-    held, xall, mine, theirs, inbox, summed, layover, guest, small_ref, smalls, half_ref, away_ref,
+    nb, phases, cuts,
+    x_in, act_in, cot_in, gamma_ref, cols_ref, weight_ref,
+    wsum_out, ret_ref, total_ref,
+    x_ref, act_ref, cot_ref, wsum_ref, held, xall, mine, theirs, inbox, summed, layover, guest, small_ref, smalls, half_ref, away_ref,
     wfull, wbf, wsend, winbox,
     line_send, line_recv, sib_send, sib_recv, own_sem, w_sem, x_send, x_on, x_recv, swap,
     pair_send, pair_recv, sum_send, lay_recv, lay_send, ret_recv, small_send, small_recv, away_sem,
-    share_send, share_recv, load_sem,
+    share_send, share_recv, load_sem, out_sem,
 ):
     rows, outs = x_ref.shape
     cols = wfull.shape[1]
     nz, per = nb // 4, nb // 2
     hz, last = nz // 2, nz - 1
-    chunks = phases * parts
-    wide = outs // chunks
+    chunks = len(cuts) - 1
+    wide = [cuts[i + 1] - cuts[i] for i in range(chunks)]
+    early, late = phases[0], phases[1]
     t, b = lax.axis_index("table"), lax.axis_index("batch")
     z, y, c = b // 4, (b // 2) % 2, b % 2
     other = 1 - t
@@ -51,7 +52,10 @@
         return pl.ds(pl.multiple_of(core * rows, rows), rows)
 
     def piece(zz, core, chunk):
-        return held.at[zz, core_rows(core), pl.ds(chunk * wide, wide)]
+        return held.at[zz, core_rows(core), pl.ds(cuts[chunk], wide[chunk])]
+
+    def outputs(ref, chunk):
+        return ref.at[pl.ds(cuts[chunk], wide[chunk]), :]
 
     def xblock(yy, zz, core):
         return xall.at[yy, zz, core_rows(core), :]
@@ -73,8 +77,6 @@
             def _():
                 act(origin(d, k))
 
-    load_w = pltpu.make_async_copy(weight_ref, wfull, load_sem)
-    load_w.start()
     barrier = pltpu.get_barrier_semaphore()
 
     def greet(tt, bb):
@@ -96,6 +98,12 @@
         lax.fori_loop(0, 2 * nz, step, 0)
 
     along(lambda i, bb: greet(t, bb))
+    loads = [
+        pltpu.make_async_copy(src, dst, load_sem.at[i])
+        for i, (src, dst) in enumerate(((act_in, act_ref), (cot_in, cot_ref), (x_in, x_ref), (weight_ref, wfull)))
+    ]
+    for load in loads:
+        load.start()
     small_ref[...] = jnp.zeros_like(small_ref)
     tall = 16 if rows % 16 == 0 else rows
     lanes = 512 if outs % 512 == 0 else outs
@@ -116,59 +124,64 @@
             small_ref[1:2, to] += jnp.sum(hidden * act * act * slope, axis=0, keepdims=True)
         return carry
 
-    lax.fori_loop(0, rows // tall, gate, 0)
-    load_w.wait()
-    wbf[y] = wfull[...].astype(BF16)
-    pl.semaphore_wait(barrier, 2 * nz + 1)
-
     def give_own(d, phase):
         @pl.when(goes[d])
         def _():
-            for chunk in range(phase * parts, phase * parts + parts):
+            for chunk in phases[phase]:
                 here = piece(z, c, chunk)
                 send(here, here, line_send.at[d, 0, chunk], line_recv.at[d, 0, chunk], t, ahead[d])
 
+    odd = c == 1
+    side = jnp.where(odd, other, t)
+
+    def target(j):
+        return device(side * hz + j // 4, y, j % 2)
+
+    def give_columns(source, chosen):
+        def give(j, carry):
+            bb = target(j)
+            there = xblock((j // 2) % 2, z, c)
+            rsem = x_recv.at[(j // 2) % 2, z, c]
+
+            @pl.when(chosen(side * hz + j // 4))
+            def _():
+                @pl.when(bb == b)
+                def _():
+                    pltpu.make_async_copy(features(source, j), there, rsem).start()
+
+                @pl.when(bb != b)
+                def _():
+                    send(features(source, j), there, x_send.at[j], rsem, t, bb)
+
+            return carry
+
+        lax.fori_loop(0, per, give, 0)
+
+    for load in loads[:3]:
+        load.wait()
+    lax.fori_loop(0, rows // tall, gate, 0)
+    loads[3].wait()
+    wbf[y] = wfull[...].astype(BF16)
+    smalls[2 * z + c] = small_ref[...]
+    pl.semaphore_wait(barrier, 2 * nz + 1)
     give_own(0, 0)
     give_own(1, 0)
     own_rows = held.at[z, core_rows(c), :]
     send(own_rows, own_rows, own_sem.at[0], own_sem.at[1], t, sibling)
-    send(wbf.at[y], wbf.at[y], w_sem.at[0], w_sem.at[1], t, across)
-
-    odd = c == 1
-    side = jnp.where(odd, other, t)
-
-    def target(j):
-        return device(side * hz + j // 4, y, j % 2)
-
-    def give_columns(source):
-        def give(i, carry):
-            j = (i + column(z, 0, c)) % per
-            bb = target(j)
-            there = xblock((j // 2) % 2, z, c)
-            rsem = x_recv.at[(j // 2) % 2, z, c]
-
-            @pl.when(bb == b)
-            def _():
-                pltpu.make_async_copy(features(source, j), there, rsem).start()
-
-            @pl.when(bb != b)
-            def _():
-                send(features(source, j), there, x_send.at[j], rsem, t, bb)
-
-            return carry
-
-        lax.fori_loop(0, per, give, 0)
 
     @pl.when(odd)
     def _():
         send(cols_ref, guest, swap.at[0], swap.at[1], other, b)
 
+    send(wbf.at[y], wbf.at[y], w_sem.at[0], w_sem.at[1], t, across)
+    near = lambda zz: jnp.logical_and(zz <= z + 1, zz >= z - 1)
+    beyond = (lambda zz: zz > z + 1, lambda zz: zz < z - 1)
+
     @pl.when(jnp.logical_not(odd))
     def _():
-        give_columns(cols_ref)
+        give_columns(cols_ref, near)
 
     along(lambda i, bb: send(small_ref, smalls.at[2 * z + c], small_send.at[i], small_recv.at[2 * z + c], t, bb))
-    smalls[2 * z + c] = small_ref[...]
     lands = (home + t) % 2
 
     def pass_columns(zz):
@@ -224,12 +237,12 @@
     group = 4 if nz % 4 == 0 else nz
 
     def product(chunk, yy):
-        to = pl.ds(chunk * wide, wide)
+        to = pl.ds(cuts[chunk], wide[chunk])
         total = None
         for g in range(0, nz, group):
             zs = pl.ds(g, group)
             term = lax.dot_general(
-                held[zs, :, to].reshape(group * 2 * rows, wide),
+                held[zs, :, to].reshape(group * 2 * rows, wide[chunk]),
                 xall[yy, zs].reshape(group * 2 * rows, cols),
                 (((0,), (0,)), ((), ())),
                 preferred_element_type=F32,
@@ -238,14 +251,14 @@
         return total
 
     def give_share(chunk):
-        wsend[chunk] = product(chunk, 1 - y).astype(BF16)
-        send(wsend.at[chunk], winbox.at[chunk], share_send.at[chunk], share_recv.at[chunk], t, across)
+        outputs(wsend, chunk)[...] = product(chunk, 1 - y).astype(BF16)
+        send(outputs(wsend, chunk), outputs(winbox, chunk), share_send.at[chunk], share_recv.at[chunk], t, across)
 
     def keep_share(chunk):
-        wsum_ref[pl.ds(chunk * wide, wide), :] = product(chunk, y)
-
-    def hop(phase, k):
-        for chunk in range(phase * parts, phase * parts + parts):
+        outputs(wsum_ref, chunk)[...] = product(chunk, y)
+
+    def hop(phase, k, then):
+        for chunk in phases[phase]:
             for d in range(2):
                 @pl.when(k < came[d])
                 def _():
@@ -258,62 +271,85 @@
 
                     send(here, here, sib_send.at[d, k, chunk], sib_recv.at[d, k, chunk], t, sibling)
 
-        if phase + 1 < phases:
             for d in range(2):
-                @pl.when(k == came[d])
-                def _():
-                    give_own(d, phase + 1)
-
-    def meet(phase, k):
+                @pl.when(k < came[d])
+                def _():
+                    done(piece(origin(d, k), 1 - c, chunk), sib_recv.at[d, k, chunk])
+
+            then(chunk)
+
+    def gather(k, carry):
+        hop(0, k, lambda chunk: None)
+
+        @pl.when(jnp.logical_and(k == 0, odd))
+        def _():
+            done(guest, swap.at[1])
+            give_columns(guest, near)
+
         for d in range(2):
-            @pl.when(k < came[d])
+            @pl.when(k == came[d])
             def _():
-                for chunk in range(phase * parts, phase * parts + parts):
-                    done(piece(origin(d, k), 1 - c, chunk), sib_recv.at[d, k, chunk])
-
-    for phase in range(phases - 1):
-        def gather(k, carry):
-            hop(phase, k)
-            if phase == 0:
-                @pl.when(k == 0)
-                def _():
-                    @pl.when(odd)
-                    def _():
-                        done(guest, swap.at[1])
-                        give_columns(guest)
-
-                    pass_columns(z)
-
-                each(k, pass_columns)
-            meet(phase, k)
-            return carry
-
-        lax.fori_loop(0, last, gather, 0)
+                @pl.when(odd)
+                def _():
+                    give_columns(guest, beyond[d])
+
+                @pl.when(jnp.logical_not(odd))
+                def _():
+                    give_columns(cols_ref, beyond[d])
+
+                give_own(d, 1)
+
+        @pl.when(k == min(1, last - 1))
+        def _():
+            pass_columns(z)
+            each(0, pass_columns)
+
+        return carry
+
+    lax.fori_loop(0, last, gather, 0)
+
+    def rest(i, carry):
+        each(i, pass_columns)
+        return carry
+
+    lax.fori_loop(1, last, rest, 0)
     along(lambda i, bb: done(smalls.at[i], small_recv.at[i]))
     half_ref[...] = jnp.sum(smalls[...], axis=0)
     send(half_ref, away_ref, away_sem.at[0], away_sem.at[1], t, across)
-    theirs_rows = held.at[z, core_rows(1 - c), :]
-    done(theirs_rows, own_sem.at[1])
-    done(wbf.at[1 - y], w_sem.at[1])
-    multiply(z)
-
-    early = chunks - parts
+    done(held.at[z, core_rows(1 - c), :], own_sem.at[1])
 
     def finish(k, carry):
-        hop(phases - 1, k)
-        meet(phases - 1, k)
+        def then(chunk):
+            if chunk < chunks - 1:
+                @pl.when(k == last - 1)
+                def _():
+                    give_share(chunk)
+
+        hop(1, k, then)
+
+        @pl.when(k == 0)
+        def _():
+            take_columns()
+            for chunk in early:
+                give_share(chunk)
+            done(wbf.at[1 - y], w_sem.at[1])
+            multiply(z)
+
         each(k, multiply)
 
-        @pl.when(k == 0)
+        @pl.when(k == last - 1)
+        def _():
+            give_share(chunks - 1)
+
+        @pl.when(k == min(1, last - 1))
         def _():
             give_sum(z)
-            take_columns()
 
         @pl.when(k > 0)
         def _():
             each(k - 1, give_sum)
 
-        @pl.when(k == 1)
+        @pl.when(k == 2)
         def _():
             pass_sum(z)
 
@@ -321,37 +357,36 @@
         def _():
             each(k - 2, pass_sum)
 
-        for chunk in range(early):
-            @pl.when(k == min(chunk, last - 1))
-            def _():
-                give_share(chunk)
-                keep_share(chunk)
-
         return carry
 
     lax.fori_loop(0, last, finish, 0)
-    for chunk in range(early, chunks):
-        give_share(chunk)
     each(last - 1, give_sum)
-    if last == 1:
+    for chunk in early:
+        keep_share(chunk)
+    if last < 3:
         pass_sum(z)
-    else:
+    if last > 1:
         each(last - 2, pass_sum)
-    for chunk in range(early, chunks):
+    for chunk in late:
         keep_share(chunk)
     each(last - 1, pass_sum)
+    keeps = []
     for chunk in range(chunks):
-        done(winbox.at[chunk], share_recv.at[chunk])
-        wsum_ref[pl.ds(chunk * wide, wide), :] += winbox[chunk].astype(F32)
+        done(outputs(winbox, chunk), share_recv.at[chunk])
+        outputs(wsum_ref, chunk)[...] += outputs(winbox, chunk)[...].astype(F32)
+        keeps.append(pltpu.make_async_copy(outputs(wsum_ref, chunk), outputs(wsum_out, chunk), out_sem.at[chunk]))
+        keeps[-1].start()
     done(away_ref, away_sem.at[1])
     total_ref[...] = half_ref[...] + away_ref[...]
+    for keep in keeps:
+        keep.wait()
 
     along(lambda i, bb: done(small_ref, small_send.at[i]))
     done(half_ref, away_sem.at[0])
     done(own_rows, own_sem.at[0])
     done(wbf.at[y], w_sem.at[0])
     for chunk in range(chunks):
-        done(wsend.at[chunk], share_send.at[chunk])
+        done(outputs(wsend, chunk), share_send.at[chunk])
 
     @pl.when(odd)
     def _():
@@ -411,21 +446,25 @@
     cols = weight.shape[1]
     nz, per = nb // 4, nb // 2
     last = nz - 1
-    phases, parts = 2, 2
-    chunks = phases * parts
-    wide = outs // chunks
+    phases, cuts = ((0, 1), (2, 3)), tuple(outs * i // 4 for i in range(5))
+    chunks = len(cuts) - 1
     dma = pltpu.SemaphoreType.DMA
     vmem = pl.BlockSpec(memory_space=pltpu.VMEM)
+    far = pl.BlockSpec(memory_space=pl.ANY)
     return pl.pallas_call(
-        functools.partial(exchange, nb, phases, parts),
+        functools.partial(exchange, nb, phases, cuts),
         out_shape=(
             jax.ShapeDtypeStruct((outs, cols), F32),
             jax.ShapeDtypeStruct(columns.shape, BF16),
             jax.ShapeDtypeStruct((2, outs), F32),
         ),
-        in_specs=[vmem] * 5 + [pl.BlockSpec(memory_space=pl.ANY)],
-        out_specs=(vmem,) * 3,
+        in_specs=[far, far, far, vmem, far, far],
+        out_specs=(far, far, vmem),
         scratch_shapes=[
+            pltpu.VMEM((rows, outs), BF16),
+            pltpu.VMEM((rows, outs), BF16),
+            pltpu.VMEM((rows, outs), BF16),
+            pltpu.VMEM((outs, cols), F32),
             pltpu.VMEM((nz, 2 * rows, outs), BF16),
             pltpu.VMEM((2, nz, 2 * rows, cols), BF16),
             pltpu.VMEM((nz, 2, rows, cols), F32),
@@ -440,8 +479,8 @@
             pltpu.VMEM((2, outs), F32),
             pltpu.VMEM((outs, cols), F32),
             pltpu.VMEM((2, outs, cols), BF16),
-            pltpu.VMEM((chunks, wide, cols), BF16),
-            pltpu.VMEM((chunks, wide, cols), BF16),
+            pltpu.VMEM((outs, cols), BF16),
+            pltpu.VMEM((outs, cols), BF16),
             dma((2, last, chunks)),
             dma((2, last, chunks)),
             dma((2, last, chunks)),
@@ -463,7 +502,8 @@
             dma((2,)),
             dma((chunks,)),
             dma((chunks,)),
-            dma,
+            dma((4,)),
+            dma((chunks,)),
         ],
         compiler_params=pltpu.CompilerParams(
             collective_id=0, has_side_effects=True, vmem_limit_bytes=60 * 1024 * 1024
@@ -484,7 +524,7 @@
 def write_results(pre_act, cotangent, gamma, share, wsum, total):
     rows, outs = pre_act.shape
     cols = wsum.shape[1]
-    steps = 4 if rows % 64 == 0 and outs % 32 == 0 else 1
+    steps = 2 if rows % 32 == 0 and outs % 16 == 0 else 1
     some = pl.BlockSpec((rows // steps, outs), lambda i: (i, 0))
     tile = pl.BlockSpec((outs // steps, cols), lambda i: (i, 0))
     whole = lambda n: pl.BlockSpec((n, outs), lambda i: (0, 0))

time: 84 us -> 80 us (0.952); the launches traced: 83.8 us -> 78.4 us
  Pallas kernels: 83.1 us -> 77.8 us
    pallas_call x1, Pallas kernels: 78.8 us -> 74.4 us  [run_exchange(): pl.pallas_call(functools.partial(exchange, nb, phases, cuts), out_shape=(...]
    pallas_call x1, Pallas kernels: 4.37 us -> 3.42 us  [write_results(): pl.pallas_call(results, grid=(steps,), out_shape=(wide, wide, jax.ShapeDt...]
where the time goes in v2:
time: 80 us; the launch traced here: 78.4 us
  Pallas kernels  77.8 us (97%)
    pallas_call x1, Pallas kernels, run_exchange(): pl.pallas_call(functools.partial(exchange, nb, phases, cuts), out_shape=(...  74.4 us
    pallas_call x1, Pallas kernels, write_results(): pl.pallas_call(results, grid=(steps,), out_shape=(wide, wide, jax.ShapeDt...  3.42 us

profile of v2, /device:TPU:3, one launch (start us, length us, event | category | flops | bytes accessed | tf_op | source)
XLA Modules:
  0.0 78.4 jit_solution(9917797686930296669)
XLA Ops:
  0.6 74.4 %shard_map.101 = (f32[2048,256]{1,0:T(8,128)}, bf16[128,2048]{1,0:T(8,128)(2,1)}, f32[2,2048]{1,0:T(2,128)}) custom-call(bf16[128,2048]{1,0:T(8,128)(2,1)} %x_in.1, bf16[128,2048]{1,0:T(8,128)(2,1)} %act_ref.1, bf16[128,2048]{1,0:T(8,128)(2,1)} %cot_ref.1, f32[1,2048]{1,0:T(1,128)} %bitcast.3, bf16[128,2048]{1,0:T(8,128)(2,1)} %cols_ref.1, ...), custom_call_target="tpu_custom_call" | custom-call | tf_op jit(solution)/shard_map/pallas_call | solution.py:454
  75.0 3.4 %shard_map.102 = (bf16[128,2048]{1,0:T(8,128)(2,1)}, bf16[128,2048]{1,0:T(8,128)(2,1)}, f32[2048,256]{1,0:T(8,128)}, f32[1,2048]{1,0:T(1,128)}, f32[1,2048]{1,0:T(1,128)}) custom-call(bf16[128,2048]{1,0:T(8,128)(2,1)} %act_ref.1, bf16[128,2048]{1,0:T(8,128)(2,1)} %cot_ref.1, f32[1,2048]{1,0:T(1,128)} %bitcast.4, ...), custom_call_target="tpu_custom_call" | custom-call | tf_op jit(solution)/shard_map/pallas_call | solution.py:533

commit v3 on v2

--- a/solution.py
+++ b/solution.py
@@ -177,10 +177,6 @@
     near = lambda zz: jnp.logical_and(zz <= z + 1, zz >= z - 1)
     beyond = (lambda zz: zz > z + 1, lambda zz: zz < z - 1)
 
-    @pl.when(jnp.logical_not(odd))
-    def _():
-        give_columns(cols_ref, near)
-
     along(lambda i, bb: send(small_ref, smalls.at[2 * z + c], small_send.at[i], small_recv.at[2 * z + c], t, bb))
     lands = (home + t) % 2
 
@@ -286,17 +282,23 @@
             done(guest, swap.at[1])
             give_columns(guest, near)
 
+        @pl.when(jnp.logical_and(k == 0, jnp.logical_not(odd)))
+        def _():
+            give_columns(cols_ref, near)
+
         for d in range(2):
+            @pl.when(k == jnp.maximum(came[d], min(1, last - 1)))
+            def _():
+                @pl.when(odd)
+                def _():
+                    give_columns(guest, beyond[d])
+
+                @pl.when(jnp.logical_not(odd))
+                def _():
+                    give_columns(cols_ref, beyond[d])
+
             @pl.when(k == came[d])
             def _():
-                @pl.when(odd)
-                def _():
-                    give_columns(guest, beyond[d])
-
-                @pl.when(jnp.logical_not(odd))
-                def _():
-                    give_columns(cols_ref, beyond[d])
-
                 give_own(d, 1)
 
         @pl.when(k == min(1, last - 1))
@@ -318,6 +320,9 @@
     send(half_ref, away_ref, away_sem.at[0], away_sem.at[1], t, across)
     done(held.at[z, core_rows(1 - c), :], own_sem.at[1])
 
+    done(wbf.at[1 - y], w_sem.at[1])
+    multiply(z)
+
     def finish(k, carry):
         def then(chunk):
             if chunk < chunks - 1:
@@ -332,8 +337,6 @@
             take_columns()
             for chunk in early:
                 give_share(chunk)
-            done(wbf.at[1 - y], w_sem.at[1])
-            multiply(z)
 
         each(k, multiply)
 

time: 80 us -> 77.8 us (0.972); the launches traced: 78.4 us -> 77.6 us
    pallas_call x1, Pallas kernels: 74.4 us -> 73.6 us  [run_exchange(): pl.pallas_call(functools.partial(exchange, nb, phases, cuts), out_shape=(...]
where the time goes in v3:
time: 77.8 us; the launch traced here: 77.6 us
  Pallas kernels  77 us (99%)
    pallas_call x1, Pallas kernels, run_exchange(): pl.pallas_call(functools.partial(exchange, nb, phases, cuts), out_shape=(...  73.6 us
    pallas_call x1, Pallas kernels, write_results(): pl.pallas_call(results, grid=(steps,), out_shape=(wide, wide, jax.ShapeDt...  3.42 us

profile of v3, /device:TPU:3, one launch (start us, length us, event | category | flops | bytes accessed | tf_op | source)
XLA Modules:
  0.0 77.6 jit_solution(6107057479235621133)
XLA Ops:
  0.6 73.6 %shard_map.101 = (f32[2048,256]{1,0:T(8,128)}, bf16[128,2048]{1,0:T(8,128)(2,1)}, f32[2,2048]{1,0:T(2,128)}) custom-call(bf16[128,2048]{1,0:T(8,128)(2,1)} %x_in.1, bf16[128,2048]{1,0:T(8,128)(2,1)} %act_ref.1, bf16[128,2048]{1,0:T(8,128)(2,1)} %cot_ref.1, f32[1,2048]{1,0:T(1,128)} %bitcast.3, bf16[128,2048]{1,0:T(8,128)(2,1)} %cols_ref.1, ...), custom_call_target="tpu_custom_call" | custom-call | tf_op jit(solution)/shard_map/pallas_call | solution.py:457
  74.2 3.4 %shard_map.102 = (bf16[128,2048]{1,0:T(8,128)(2,1)}, bf16[128,2048]{1,0:T(8,128)(2,1)}, f32[2048,256]{1,0:T(8,128)}, f32[1,2048]{1,0:T(1,128)}, f32[1,2048]{1,0:T(1,128)}) custom-call(bf16[128,2048]{1,0:T(8,128)(2,1)} %act_ref.1, bf16[128,2048]{1,0:T(8,128)(2,1)} %cot_ref.1, f32[1,2048]{1,0:T(1,128)} %bitcast.4, ...), custom_call_target="tpu_custom_call" | custom-call | tf_op jit(solution)/shard_map/pallas_call | solution.py:536

commit v4 on v3

--- a/solution.py
+++ b/solution.py
@@ -16,10 +16,10 @@
     nb, phases, cuts,
     x_in, act_in, cot_in, gamma_ref, cols_ref, weight_ref,
     wsum_out, ret_ref, total_ref,
-    x_ref, act_ref, cot_ref, wsum_ref, held, xall, mine, theirs, inbox, summed, layover, guest, small_ref, smalls, half_ref, away_ref,
+    x_ref, act_ref, cot_ref, wsum_ref, held, xall, mine, theirs, inbox, summed, layover, guest, small_ref, smalls, half_ref, near_ref, both_ref, away_ref,
     wfull, wbf, wsend, winbox,
     line_send, line_recv, sib_send, sib_recv, own_sem, w_sem, x_send, x_on, x_recv, swap,
-    pair_send, pair_recv, sum_send, lay_recv, lay_send, ret_recv, small_send, small_recv, away_sem,
+    pair_send, pair_recv, sum_send, lay_recv, lay_send, ret_recv, small_send, small_recv, near_sem, away_sem,
     share_send, share_recv, load_sem, out_sem,
 ):
     rows, outs = x_ref.shape
@@ -162,7 +162,7 @@
     lax.fori_loop(0, rows // tall, gate, 0)
     loads[3].wait()
     wbf[y] = wfull[...].astype(BF16)
-    smalls[2 * z + c] = small_ref[...]
+    smalls[z] = small_ref[...]
     pl.semaphore_wait(barrier, 2 * nz + 1)
     give_own(0, 0)
     give_own(1, 0)
@@ -177,7 +177,17 @@
     near = lambda zz: jnp.logical_and(zz <= z + 1, zz >= z - 1)
     beyond = (lambda zz: zz > z + 1, lambda zz: zz < z - 1)
 
-    along(lambda i, bb: send(small_ref, smalls.at[2 * z + c], small_send.at[i], small_recv.at[2 * z + c], t, bb))
+    def same_core(act):
+        def step(zz, carry):
+            @pl.when(zz != z)
+            def _():
+                act(zz, device(zz, y, c))
+
+            return carry
+
+        lax.fori_loop(0, nz, step, 0)
+
+    same_core(lambda zz, bb: send(small_ref, smalls.at[z], small_send.at[zz], small_recv.at[z], t, bb))
     lands = (home + t) % 2
 
     def pass_columns(zz):
@@ -315,9 +325,9 @@
         return carry
 
     lax.fori_loop(1, last, rest, 0)
-    along(lambda i, bb: done(smalls.at[i], small_recv.at[i]))
+    same_core(lambda zz, bb: done(smalls.at[zz], small_recv.at[zz]))
     half_ref[...] = jnp.sum(smalls[...], axis=0)
-    send(half_ref, away_ref, away_sem.at[0], away_sem.at[1], t, across)
+    send(half_ref, near_ref, near_sem.at[0], near_sem.at[1], t, sibling)
     done(held.at[z, core_rows(1 - c), :], own_sem.at[1])
 
     done(wbf.at[1 - y], w_sem.at[1])
@@ -363,6 +373,9 @@
         return carry
 
     lax.fori_loop(0, last, finish, 0)
+    done(near_ref, near_sem.at[1])
+    both_ref[...] = half_ref[...] + near_ref[...]
+    send(both_ref, away_ref, away_sem.at[0], away_sem.at[1], t, across)
     each(last - 1, give_sum)
     for chunk in early:
         keep_share(chunk)
@@ -380,12 +393,13 @@
         keeps.append(pltpu.make_async_copy(outputs(wsum_ref, chunk), outputs(wsum_out, chunk), out_sem.at[chunk]))
         keeps[-1].start()
     done(away_ref, away_sem.at[1])
-    total_ref[...] = half_ref[...] + away_ref[...]
+    total_ref[...] = both_ref[...] + away_ref[...]
     for keep in keeps:
         keep.wait()
 
-    along(lambda i, bb: done(small_ref, small_send.at[i]))
-    done(half_ref, away_sem.at[0])
+    same_core(lambda zz, bb: done(small_ref, small_send.at[zz]))
+    done(half_ref, near_sem.at[0])
+    done(both_ref, away_sem.at[0])
     done(own_rows, own_sem.at[0])
     done(wbf.at[y], w_sem.at[0])
     for chunk in range(chunks):
@@ -477,7 +491,9 @@
             pltpu.VMEM((per, rows, cols), BF16),
             pltpu.VMEM(columns.shape, BF16),
             pltpu.VMEM((2, outs), F32),
-            pltpu.VMEM((2 * nz, 2, outs), F32),
+            pltpu.VMEM((nz, 2, outs), F32),
+            pltpu.VMEM((2, outs), F32),
+            pltpu.VMEM((2, outs), F32),
             pltpu.VMEM((2, outs), F32),
             pltpu.VMEM((2, outs), F32),
             pltpu.VMEM((outs, cols), F32),
@@ -500,8 +516,9 @@
             dma((per,)),
             dma((per,)),
             dma((per,)),
-            dma((2 * nz,)),
-            dma((2 * nz,)),
+            dma((nz,)),
+            dma((nz,)),
+            dma((2,)),
             dma((2,)),
             dma((chunks,)),
             dma((chunks,)),

time: 77.8 us -> 77.1 us (level)
  Pallas kernels: 77 us -> 76.1 us
    pallas_call x1, Pallas kernels: 73.6 us -> 72.7 us  [run_exchange(): pl.pallas_call(functools.partial(exchange, nb, phases, cuts), out_shape=(...]
where the time goes in v4:
time: 77.1 us; the launch traced here: 76.7 us
  Pallas kernels  76.1 us (99%)
    pallas_call x1, Pallas kernels, run_exchange(): pl.pallas_call(functools.partial(exchange, nb, phases, cuts), out_shape=(...  72.7 us
    pallas_call x1, Pallas kernels, write_results(): pl.pallas_call(results, grid=(steps,), out_shape=(wide, wide, jax.ShapeDt...  3.42 us

profile of v4, /device:TPU:3, one launch (start us, length us, event | category | flops | bytes accessed | tf_op | source)
XLA Modules:
  0.0 76.7 jit_solution(10363814034353027167)
XLA Ops:
  0.6 72.7 %shard_map.101 = (f32[2048,256]{1,0:T(8,128)}, bf16[128,2048]{1,0:T(8,128)(2,1)}, f32[2,2048]{1,0:T(2,128)}) custom-call(bf16[128,2048]{1,0:T(8,128)(2,1)} %x_in.1, bf16[128,2048]{1,0:T(8,128)(2,1)} %act_ref.1, bf16[128,2048]{1,0:T(8,128)(2,1)} %cot_ref.1, f32[1,2048]{1,0:T(1,128)} %bitcast.3, bf16[128,2048]{1,0:T(8,128)(2,1)} %cols_ref.1, ...), custom_call_target="tpu_custom_call" | custom-call | tf_op jit(solution)/shard_map/pallas_call | solution.py:471
  73.3 3.4 %shard_map.102 = (bf16[128,2048]{1,0:T(8,128)(2,1)}, bf16[128,2048]{1,0:T(8,128)(2,1)}, f32[2048,256]{1,0:T(8,128)}, f32[1,2048]{1,0:T(1,128)}, f32[1,2048]{1,0:T(1,128)}) custom-call(bf16[128,2048]{1,0:T(8,128)(2,1)} %act_ref.1, bf16[128,2048]{1,0:T(8,128)(2,1)} %cot_ref.1, f32[1,2048]{1,0:T(1,128)} %bitcast.4, ...), custom_call_target="tpu_custom_call" | custom-call | tf_op jit(solution)/shard_map/pallas_call | solution.py:553

commit v5 on v4

--- a/solution.py
+++ b/solution.py
@@ -342,13 +342,13 @@
 
         hop(1, k, then)
 
+        each(k, multiply)
+
         @pl.when(k == 0)
         def _():
             take_columns()
             for chunk in early:
                 give_share(chunk)
-
-        each(k, multiply)
 
         @pl.when(k == last - 1)
         def _():

time: 77.1 us -> 78 us (1.012); the launches traced: 76.7 us -> 76.7 us
  no operation moved by 1% of the time
where the time goes in v5:
time: 78 us; the launch traced here: 76.7 us
  Pallas kernels  76 us (97%)
    pallas_call x1, Pallas kernels, run_exchange(): pl.pallas_call(functools.partial(exchange, nb, phases, cuts), out_shape=(...  72.6 us
    pallas_call x1, Pallas kernels, write_results(): pl.pallas_call(results, grid=(steps,), out_shape=(wide, wide, jax.ShapeDt...  3.42 us

profile of v5, /device:TPU:3, one launch (start us, length us, event | category | flops | bytes accessed | tf_op | source)
XLA Modules:
  0.0 76.7 jit_solution(15723256331267979754)
XLA Ops:
  0.6 72.6 %shard_map.101 = (f32[2048,256]{1,0:T(8,128)}, bf16[128,2048]{1,0:T(8,128)(2,1)}, f32[2,2048]{1,0:T(2,128)}) custom-call(bf16[128,2048]{1,0:T(8,128)(2,1)} %x_in.1, bf16[128,2048]{1,0:T(8,128)(2,1)} %act_ref.1, bf16[128,2048]{1,0:T(8,128)(2,1)} %cot_ref.1, f32[1,2048]{1,0:T(1,128)} %bitcast.3, bf16[128,2048]{1,0:T(8,128)(2,1)} %cols_ref.1, ...), custom_call_target="tpu_custom_call" | custom-call | tf_op jit(solution)/shard_map/pallas_call | solution.py:471
  73.3 3.4 %shard_map.102 = (bf16[128,2048]{1,0:T(8,128)(2,1)}, bf16[128,2048]{1,0:T(8,128)(2,1)}, f32[2048,256]{1,0:T(8,128)}, f32[1,2048]{1,0:T(1,128)}, f32[1,2048]{1,0:T(1,128)}) custom-call(bf16[128,2048]{1,0:T(8,128)(2,1)} %act_ref.1, bf16[128,2048]{1,0:T(8,128)(2,1)} %cot_ref.1, f32[1,2048]{1,0:T(1,128)} %bitcast.4, ...), custom_call_target="tpu_custom_call" | custom-call | tf_op jit(solution)/shard_map/pallas_call | solution.py:553
